TPU v7x, 32 devices: a whole 2x2x4 slice. The times are simulated.
32 devices in a mesh: rep: 4 (over y, x), shard: 8 (over z, core).
Axes of the slice: x: 2, y: 2, z: 4, core: 2. Of those that a mesh axis runs over, the one named last changes fastest.
Arguments:
- tokens: bfloat16 [2, 32, 1024, 768], P(None, ('rep', 'shard')), may hold values from -6 to 6
- cotangent: bfloat16 [2, 32, 1024, 768], P(None, ('rep', 'shard')), may hold values from -6 to 6
- timestep: int32 [2, 32], P(None, ('rep', 'shard')), may hold values from 0 to 1023
- seg_lengths: int32 [2, 32, 12], P(None, ('rep', 'shard')), may hold values from 1 to 128, 768 in all within a row
- attn_gain: bfloat16 [768], P('shard'), may hold values from 0.099609375 to 1.8984375
- w_qkv: bfloat16 [768, 2304], P('shard'), may hold values from -0.3125 to 0.3125
- w_out: bfloat16 [768, 768], P('shard'), may hold values from -1.25 to 1.25
- mlp_gain: bfloat16 [768], P('shard'), may hold values from 0.099609375 to 1.8984375
- w_up: bfloat16 [768, 3072], P('shard'), may hold values from -0.21875 to 0.21875
- b_up: bfloat16 [3072], P('shard'), may hold values from -3 to 3
- w_down: bfloat16 [3072, 768], P('shard'), may hold values from -0.109375 to 0.109375
- b_down: bfloat16 [768], P('shard'), may hold values from -3 to 3
- w_mod: bfloat16 [128, 4608], P(None, 'shard'), may hold values from -0.5 to 0.5
- b_mod: bfloat16 [4608], P('shard'), may hold values from -3 to 3
Outputs:
- output: bfloat16 [2, 32, 1024, 768], P(None, ('rep', 'shard'))
- input_grad: bfloat16 [2, 32, 1024, 768], P(None, ('rep', 'shard'))
- grad_attn_gain: float32 [768], P('shard')
- grad_w_qkv: float32 [768, 2304], P('shard')
- grad_w_out: float32 [768, 768], P('shard')
- grad_mlp_gain: float32 [768], P('shard')
- grad_w_up: float32 [768, 3072], P('shard')
- grad_b_up: float32 [3072], P('shard')
- grad_w_down: float32 [3072, 768], P('shard')
- grad_b_down: float32 [768], P('shard')
- grad_w_mod: float32 [128, 4608], P(None, 'shard')
- grad_b_mod: float32 [4608], P('shard')
Inputs may be any that keep to these rules, and one draw needn't show every extreme that they name: `seg_lengths`: the twelve lengths of each tree sum to 768.
All inputs are finite; a program needn't handle non-finite values.
Results may differ from a plain program's by a relative error of at most 0.015.
The roundings to bfloat16 on the way count: a program that leaves them out, or rounds other values in their place, can miss the bound.
Values may be sent and summed in bfloat16 or wider, within the bound.
A program may use at most 256 MiB of HBM per device.

v0:
```python
import math

import jax
import jax.numpy as jnp
from jax import lax
from jax.sharding import PartitionSpec as P

D = 768
HEADS = 12
HD = 64
COND = 128
TRUNK = 256
TLEN = 1024
QBLOCK = 512


HIGHEST = lax.Precision.HIGHEST


def as_sent(array):
    return jax.tree.map(lambda a: a.astype(jnp.bfloat16) if a.dtype == jnp.float32 else a, array)


def time_cond(indices):
    halfway = COND // 2
    frequency = jnp.exp(-math.log(10000.0) * jnp.arange(halfway, dtype=jnp.float32) / halfway)
    angles = indices.astype(jnp.float32)[..., None] * frequency
    return jax.nn.silu(jnp.concatenate([jnp.cos(angles), jnp.sin(angles)], axis=-1))


def segment_ids(length_row):
    bounds = jnp.cumsum(length_row, dtype=jnp.int32)
    places = jnp.arange(TLEN, dtype=jnp.int32)
    offset = places - TRUNK
    inside = jnp.sum(
        (offset[:, None] >= bounds[None, :]).astype(jnp.int32), axis=1, dtype=jnp.int32
    )
    return jnp.where(places < TRUNK, 0, 1 + inside)


def path_mask(segment):
    parent = jnp.where(segment >= 5, 1 + (segment - 5) // 2, 0)
    keyseg = segment[None, :]
    return (keyseg == 0) | (keyseg == segment[:, None]) | (keyseg == parent[:, None])


def modulated_norm(values, gain_vec, shift_vec, scale_vec):
    center = values - jnp.mean(values, axis=-1, keepdims=True)
    spread = jnp.mean(center * center, axis=-1, keepdims=True)
    return center * lax.rsqrt(spread + 1e-05) * gain_vec * (1.0 + scale_vec) + shift_vec


def gelu_tanh(values):
    return jax.nn.gelu(values, approximate=True)


def split_heads(proj_qkv):
    queries = proj_qkv[:, :D].reshape(TLEN, HEADS, HD)
    keys_all = proj_qkv[:, D : 2 * D].reshape(TLEN, HEADS, HD)
    values_all = proj_qkv[:, 2 * D :].reshape(TLEN, HEADS, HD)
    return (queries, keys_all, values_all)


def attention_forward(inputs):
    proj_qkv, length_row = inputs
    allowed = path_mask(segment_ids(length_row))
    factor = 1.0 / math.sqrt(HD)
    queries, keys_all, values_all = split_heads(proj_qkv)
    outputs_list = []
    log_list = []
    for row_start in range(0, TLEN, QBLOCK):
        scores = (
            jnp.einsum(
                "qhd,khd->hqk",
                queries[row_start : row_start + QBLOCK],
                keys_all,
                preferred_element_type=jnp.float32,
            )
            * factor
        )
        scores = jnp.where(allowed[None, row_start : row_start + QBLOCK, :], scores, -1e30)
        maxima = jnp.max(scores, axis=-1, keepdims=True)
        exponent = jnp.exp(scores - maxima)
        totals = jnp.sum(exponent, axis=-1, keepdims=True)
        attn_probs = (exponent / totals).astype(jnp.bfloat16)
        mixed = jnp.einsum(
            "hqk,khd->qhd", attn_probs, values_all, preferred_element_type=jnp.float32
        )
        outputs_list.append(mixed.reshape(QBLOCK, D).astype(jnp.bfloat16))
        log_list.append((maxima + jnp.log(totals))[:, :, 0])
    return (jnp.concatenate(outputs_list, axis=0), jnp.concatenate(log_list, axis=1))


def attention_backward(inputs):
    proj_qkv, length_row, d_mixed, log_sums = inputs
    allowed = path_mask(segment_ids(length_row))
    factor = 1.0 / math.sqrt(HD)
    queries, keys_all, values_all = split_heads(proj_qkv)
    d_out = d_mixed.reshape(TLEN, HEADS, HD)
    d_keys = jnp.zeros((TLEN, HEADS, HD), jnp.float32)
    d_values = jnp.zeros((TLEN, HEADS, HD), jnp.float32)
    query_list = []
    for row_start in range(0, TLEN, QBLOCK):
        block_q = queries[row_start : row_start + QBLOCK]
        block_d = d_out[row_start : row_start + QBLOCK]
        scores = (
            jnp.einsum("qhd,khd->hqk", block_q, keys_all, preferred_element_type=jnp.float32)
            * factor
        )
        scores = jnp.where(allowed[None, row_start : row_start + QBLOCK, :], scores, -1e30)
        probs_full = jnp.exp(scores - log_sums[:, row_start : row_start + QBLOCK, None])
        probs_low = probs_full.astype(jnp.bfloat16)
        d_values = d_values + jnp.einsum(
            "hqk,qhd->khd", probs_low, block_d, preferred_element_type=jnp.float32
        )
        d_probs = jnp.einsum(
            "qhd,khd->hqk", block_d, values_all, preferred_element_type=jnp.float32
        )
        inner_sum = jnp.sum(d_probs * probs_full, axis=-1, keepdims=True)
        d_scores = (probs_full * (d_probs - inner_sum)).astype(jnp.bfloat16)
        query_list.append(
            jnp.einsum("hqk,khd->qhd", d_scores, keys_all, preferred_element_type=jnp.float32)
            * factor
        )
        d_keys = (
            d_keys
            + jnp.einsum("hqk,qhd->khd", d_scores, block_q, preferred_element_type=jnp.float32)
            * factor
        )
    d_queries = jnp.concatenate(query_list, axis=0)
    return jnp.concatenate(
        [d_queries.reshape(TLEN, D), d_keys.reshape(TLEN, D), d_values.reshape(TLEN, D)], axis=1
    ).astype(jnp.bfloat16)


def layer_pass(gathered, x_micro, cot_micro, time_micro, length_micro):
    gain_a, qkv_w, out_w, gain_m, up_w, up_b, down_w, down_b, mod_w, mod_b = gathered
    trees_here = x_micro.shape[0]
    row_total = trees_here * TLEN
    cond_rows = time_cond(time_micro).astype(jnp.bfloat16)
    modulation = jnp.dot(cond_rows, mod_w, preferred_element_type=jnp.float32) + mod_b.astype(
        jnp.float32
    )
    pieces = [modulation[:, None, number * D : (number + 1) * D] for number in range(6)]
    x_full = x_micro.astype(jnp.float32)
    hidden_a, first_pull = jax.vjp(
        modulated_norm, x_full, gain_a.astype(jnp.float32), pieces[0], pieces[1]
    )
    hidden_a_low = hidden_a.astype(jnp.bfloat16).reshape(row_total, D)
    proj_qkv = (
        jnp.dot(hidden_a_low, qkv_w, preferred_element_type=jnp.float32)
        .astype(jnp.bfloat16)
        .reshape(trees_here, TLEN, 3 * D)
    )
    mixed, log_sums = lax.map(attention_forward, (proj_qkv, length_micro))
    mixed_rows = mixed.reshape(row_total, D)
    branch = jnp.dot(mixed_rows, out_w, preferred_element_type=jnp.float32).reshape(
        trees_here, TLEN, D
    )
    middle = x_full + pieces[2] * branch
    hidden_m, second_pull = jax.vjp(
        modulated_norm, middle, gain_m.astype(jnp.float32), pieces[3], pieces[4]
    )
    hidden_m_low = hidden_m.astype(jnp.bfloat16).reshape(row_total, D)
    upward = jnp.dot(hidden_m_low, up_w, preferred_element_type=jnp.float32) + up_b.astype(
        jnp.float32
    )
    active, gelu_pull = jax.vjp(gelu_tanh, upward)
    active_low = active.astype(jnp.bfloat16)
    downward = (
        jnp.dot(active_low, down_w, preferred_element_type=jnp.float32) + down_b.astype(jnp.float32)
    ).reshape(trees_here, TLEN, D)
    output = (middle + pieces[5] * downward).astype(jnp.bfloat16)
    cot_full = cot_micro.astype(jnp.float32)
    d_gate_m = jnp.sum(cot_full * downward, axis=1)
    d_down = (cot_full * pieces[5]).astype(jnp.bfloat16).reshape(row_total, D)
    grad_b_down = jnp.sum(d_down.astype(jnp.float32), axis=0)
    grad_w_down = jnp.einsum("tf,td->fd", active_low, d_down, preferred_element_type=jnp.float32)
    (d_active,) = gelu_pull(
        jnp.einsum("td,fd->tf", d_down, down_w, preferred_element_type=jnp.float32)
    )
    d_up = d_active.astype(jnp.bfloat16)
    grad_b_up = jnp.sum(d_up.astype(jnp.float32), axis=0)
    grad_w_up = jnp.einsum("td,tf->df", hidden_m_low, d_up, preferred_element_type=jnp.float32)
    d_hidden_m = jnp.einsum("tf,df->td", d_up, up_w, preferred_element_type=jnp.float32).reshape(
        trees_here, TLEN, D
    )
    d_middle_part, grad_gain_m, d_shift_m, d_scale_m = second_pull(d_hidden_m)
    d_middle = cot_full + d_middle_part
    d_gate_a = jnp.sum(d_middle * branch, axis=1)
    d_branch = (d_middle * pieces[2]).astype(jnp.bfloat16).reshape(row_total, D)
    grad_w_out = jnp.einsum("td,te->de", mixed_rows, d_branch, preferred_element_type=jnp.float32)
    d_mixed = (
        jnp.einsum("te,de->td", d_branch, out_w, preferred_element_type=jnp.float32)
        .astype(jnp.bfloat16)
        .reshape(trees_here, TLEN, D)
    )
    d_proj = lax.map(attention_backward, (proj_qkv, length_micro, d_mixed, log_sums)).reshape(
        row_total, 3 * D
    )
    grad_w_qkv = jnp.einsum("td,te->de", hidden_a_low, d_proj, preferred_element_type=jnp.float32)
    d_hidden_a = jnp.einsum("te,de->td", d_proj, qkv_w, preferred_element_type=jnp.float32).reshape(
        trees_here, TLEN, D
    )
    d_input_part, grad_gain_a, d_shift_a, d_scale_a = first_pull(d_hidden_a)
    input_grad = (d_middle + d_input_part).astype(jnp.bfloat16)
    d_modulation = jnp.concatenate(
        [d_shift_a[:, 0], d_scale_a[:, 0], d_gate_a, d_shift_m[:, 0], d_scale_m[:, 0], d_gate_m],
        axis=1,
    )
    grad_b_mod = jnp.sum(d_modulation, axis=0)
    grad_w_mod = jnp.dot(cond_rows.astype(jnp.float32).T, d_modulation, precision=HIGHEST)
    full_grads = (
        grad_gain_a,
        grad_w_qkv,
        grad_w_out,
        grad_gain_m,
        grad_w_up,
        grad_b_up,
        grad_w_down,
        grad_b_down,
        grad_w_mod,
        grad_b_mod,
    )
    return (full_grads, output, input_grad)


def per_device(
    tokens,
    cotangent,
    timestep,
    seg_lengths,
    attn_gain,
    w_qkv,
    w_out,
    mlp_gain,
    w_up,
    b_up,
    w_down,
    b_down,
    w_mod,
    b_mod,
):
    shards = (attn_gain, w_qkv, w_out, mlp_gain, w_up, b_up, w_down, b_down, w_mod, b_mod)
    starting = tuple((jnp.zeros(weight.shape, jnp.float32) for weight in shards))

    def micro_batch(accum_grads, inputs):
        gathered = (
            lax.all_gather(shards[0], "shard", axis=0, tiled=True),
            lax.all_gather(shards[1], "shard", axis=0, tiled=True),
            lax.all_gather(shards[2], "shard", axis=0, tiled=True),
            lax.all_gather(shards[3], "shard", axis=0, tiled=True),
            lax.all_gather(shards[4], "shard", axis=0, tiled=True),
            lax.all_gather(shards[5], "shard", axis=0, tiled=True),
            lax.all_gather(shards[6], "shard", axis=0, tiled=True),
            lax.all_gather(shards[7], "shard", axis=0, tiled=True),
            lax.all_gather(shards[8], "shard", axis=1, tiled=True),
            lax.all_gather(shards[9], "shard", axis=0, tiled=True),
        )
        x_micro, cot_micro, time_micro, length_micro = inputs
        full_grads, output, input_grad = layer_pass(
            gathered, x_micro, cot_micro, time_micro, length_micro
        )
        shares = (
            lax.psum_scatter(full_grads[0], "shard", scatter_dimension=0, tiled=True),
            lax.psum_scatter(full_grads[1], "shard", scatter_dimension=0, tiled=True),
            lax.psum_scatter(full_grads[2], "shard", scatter_dimension=0, tiled=True),
            lax.psum_scatter(full_grads[3], "shard", scatter_dimension=0, tiled=True),
            lax.psum_scatter(full_grads[4], "shard", scatter_dimension=0, tiled=True),
            lax.psum_scatter(full_grads[5], "shard", scatter_dimension=0, tiled=True),
            lax.psum_scatter(full_grads[6], "shard", scatter_dimension=0, tiled=True),
            lax.psum_scatter(full_grads[7], "shard", scatter_dimension=0, tiled=True),
            lax.psum_scatter(full_grads[8], "shard", scatter_dimension=1, tiled=True),
            lax.psum_scatter(full_grads[9], "shard", scatter_dimension=0, tiled=True),
        )
        accum_grads = tuple((running + addend for running, addend in zip(accum_grads, shares)))
        return (accum_grads, (output, input_grad))

    totals, (outputs, input_grads) = lax.scan(
        micro_batch, starting, (tokens, cotangent, timestep, seg_lengths)
    )
    summed = jax.tree.map(lambda part: part.astype(jnp.float32), lax.psum(as_sent(totals), "rep"))
    return (
        outputs,
        input_grads,
        summed[0],
        summed[1],
        summed[2],
        summed[3],
        summed[4],
        summed[5],
        summed[6],
        summed[7],
        summed[8],
        summed[9],
    )


def solution(mesh):
    in_specs = (
        P(None, ("rep", "shard"), None, None),
        P(None, ("rep", "shard"), None, None),
        P(None, ("rep", "shard")),
        P(None, ("rep", "shard"), None),
        P("shard"),
        P("shard", None),
        P("shard", None),
        P("shard"),
        P("shard", None),
        P("shard"),
        P("shard", None),
        P("shard"),
        P(None, "shard"),
        P("shard"),
    )
    out_specs = (
        P(None, ("rep", "shard"), None, None),
        P(None, ("rep", "shard"), None, None),
        P("shard"),
        P("shard", None),
        P("shard", None),
        P("shard"),
        P("shard", None),
        P("shard"),
        P("shard", None),
        P("shard"),
        P(None, "shard"),
        P("shard"),
    )
    return jax.shard_map(
        per_device, mesh=mesh, in_specs=in_specs, out_specs=out_specs, check_vma=False
    )
```

profile of v0, /device:TPU:0, one launch (start us, length us, event | category | flops | bytes accessed | tf_op | source)
XLA Modules:
  0.0 1599.9 jit_solution(3527308759649815979)
XLA Ops:
  8.1 1501.5 %while.30 = (s32[]{:T(128)}, f32[96]{0:T(128)}, f32[96,2304]{1,0:T(8,128)}, f32[96,768]{1,0:T(8,128)}, f32[96]{0:T(128)}, /*index=5*/f32[96,3072]{1,0:T(8,128)},...) while((s32[]{:T(128)}, f32[96]{0:T(128)}, ...), condition=%wide.region_37.38_spmd.clone, body=%wide.region_0.37_spmd.clone.sunk | while | flops 53741711360 | bytes 1501392896 | solution.py:279
  22.1 31.0 %all-reduce.19 = (bf16[4608]{0:T(1024)(128)(2,1)S(1)}, bf16[768]{0:T(1024)(128)(2,1)S(1)}, bf16[768]{0:T(1024)(128)(2,1)S(1)}, bf16[768]{0:T(1024)(128)(2,1)S(1)}) all-reduce(bf16[4608]{0:T(1024)(128)(2,1)S(1)} %dynamic-update-slice.36, bf16[768]{0:T(1024)(128)(2,1)S(1)} %dynamic-update-slice.37, ...), channel_id=1, replica_groups=mesh['rep'=4,'shard'=8] {'shard'}, use_global_device_ids=true, to_apply=%add.1 | all-reduce | flops 6912 | bytes 27648 | tf_op jit(solution)/shard_map/while
  54.3 13.4 all-gather.3
  147.9 13.5 fusion.265
  180.0 16.4 %multiply_convert_fusion.12 = (bf16[1024,3072]{1,0:T(8,128)(2,1)}, f32[1024,3072]{1,0:T(8,128)}) fusion(f32[3072]{0:T(1024)S(1)} %bitcast.295, bf16[768,3072]{1,0:T(8,128)(2,1)} %all-gather.16.cloned.1.call-done, f32[1024,768]{0,1:T(8,128)} %copy-done.6, f32[768]{0:T(1024)S(1)} %get-tuple-element.1086, f32[768]{0:T(1024)S(1)} %get-tuple-element.1087, ...), kind=kOutput, calls=%fused_computation.27.clone.1 | convolution fusion | flops 4868014080 | bytes 26768384 | tf_op jit(solution)/shard_map/while/body/eval_jaxpr/dot_general | solution.py:165
  206.6 17.4 %convert_reduce_fusion.9 = (f32[3072]{0:T(1024)}, bf16[1024,3072]{1,0:T(8,128)(2,1)S(1)}) fusion(f32[1024,3072]{1,0:T(8,128)} %get-tuple-element.1090, f32[3072]{0:T(1024)S(1)} %bitcast.296, bf16[3072,768]{1,0:T(8,128)(2,1)} %all-gather.18.cloned.1.call-done, bf16[1,1,1024,768]{2,3,1,0:T(8,128)(2,1)S(1)} %copy-done.19, f32[768]{0:T(1024)S(1)} %copy-done.69), kind=kOutput, calls=%fused_computation.28.clone.1 | convolution fusion | flops 4906546176 | bytes 25193472 | tf_op jit(solution)/shard_map/while/body/eval_jaxpr/td,fd->tf/dot_general | solution.py:180
  244.9 21.4 %multiply_reduce_fusion.13 = (f32[12,512]{1,0:T(8,128)S(1)}, f32[12,512,1024]{2,1,0:T(8,128)}) fusion(f32[12,512]{1,0:T(8,128)S(1)} %log_add_fusion.5, f32[12,512,1024]{2,1,0:T(8,128)} %get-tuple-element.1084, pred[512,1024]{1,0:T(8,128)(4,1)S(1)} %copy-done.16, bf16[512,12,64]{0,2,1:T(8,128)(2,1)S(1)} %bitcast.288, ...), kind=kOutput, calls=%fused_computation.4.clone.1 | convolution fusion | flops 836757504 | bytes 53264384 | tf_op jit(solution)/shard_map/while/body/eval_jaxpr/while/body/eval_jaxpr/qhd,khd->hqk/dot_general | solution.py:116
  266.3 17.6 %multiply_convert_fusion.14 = bf16[12,512,1024]{2,1,0:T(8,128)(2,1)S(1)} fusion(f32[12,512,1024]{2,1,0:T(8,128)} %get-tuple-element.1099, f32[12,512]{1,0:T(8,128)S(1)} %get-tuple-element.1100, f32[12,512]{1,0:T(8,128)S(1)} %log_add_fusion.5, f32[12,512,1024]{2,1,0:T(8,128)} %get-tuple-element.1084, pred[512,1024]{1,0:T(8,128)(4,1)} %get-tuple-element.1081), kind=kLoop, calls=%fused_computation.3.clone.1 | loop fusion | flops 37748736 | bytes 63488000 | tf_op jit(solution)/shard_map/while/body/eval_jaxpr/while/body/eval_jaxpr/convert_element_type | solution.py:120
  308.6 17.8 %multiply_reduce_fusion.14 = (f32[12,512]{1,0:T(8,128)S(1)}, f32[12,512,1024]{2,1,0:T(8,128)}) fusion(f32[12,512]{1,0:T(8,128)S(1)} %log_add_fusion.4, f32[12,512,1024]{2,1,0:T(8,128)} %get-tuple-element.1080, pred[512,1024]{1,0:T(8,128)(4,1)S(1)} %copy-done.15, bf16[512,12,64]{0,2,1:T(8,128)(2,1)} %bitcast.290, bf16[1024,12,64]{0,2,1:T(8,128)(2,1)S(1)} %bitcast.280), kind=kOutput, calls=%fused_computation.1.clone.1 | convolution fusion | flops 836757504 | bytes 53264384 | tf_op jit(solution)/shard_map/while/body/eval_jaxpr/while/body/eval_jaxpr/qhd,khd->hqk/dot_general | solution.py:116
  326.4 13.9 add_convert_fusion.9
  340.3 17.2 %multiply_convert_fusion.15 = bf16[12,512,1024]{2,1,0:T(8,128)(2,1)S(1)} fusion(f32[12,512,1024]{2,1,0:T(8,128)} %get-tuple-element.1101, f32[12,512]{1,0:T(8,128)S(1)} %get-tuple-element.1102, f32[12,512]{1,0:T(8,128)S(1)} %log_add_fusion.4, f32[12,512,1024]{2,1,0:T(8,128)} %get-tuple-element.1080, pred[512,1024]{1,0:T(8,128)(4,1)} %get-tuple-element.1076), kind=kLoop, calls=%fused_computation.clone.1 | loop fusion | flops 37748736 | bytes 63488000 | tf_op jit(solution)/shard_map/while/body/eval_jaxpr/while/body/eval_jaxpr/convert_element_type | solution.py:120
  385.3 14.4 fusion.282
  448.2 28.6 %all-reduce.20 = (f32[768]{0:T(1024)}, f32[768]{0:T(1024)}, f32[3072]{0:T(1024)}, f32[768]{0:T(1024)}, f32[4608]{0:T(1024)}) all-reduce(f32[768]{0:T(1024)S(1)} %get-tuple-element.1104, f32[768]{0:T(1024)S(1)} %copy-done.62, f32[3072]{0:T(1024)S(1)} %copy-done.64, ...), channel_id=2, replica_groups=mesh['rep'=4,'shard'=8] {'shard'}, use_global_device_ids=true, to_apply=%region_16.16.clone | all-reduce | flops 9984 | bytes 79872 | tf_op jit(solution)/shard_map/while
  485.0 72.7 %reduce-scatter.10.cloned.1.call-done = f32[96,2304]{1,0:T(8,128)} async-done(((f32[768,2304]{1,0:T(8,128)}), f32[96,2304]{1,0:T(8,128)}) %reduce-scatter.10.cloned.1.call-update) | async-done | bytes 884752 | tf_op jit(solution)/shard_map/while/body/eval_jaxpr/reduce_scatter | solution.py:266
  559.1 98.8 %reduce-scatter.14.cloned.1.call-done = f32[96,3072]{1,0:T(8,128)} async-done(((f32[768,3072]{1,0:T(8,128)}), f32[96,3072]{1,0:T(8,128)}) %reduce-scatter.14.cloned.1.call-update) | async-done | bytes 1179664 | tf_op jit(solution)/shard_map/while/body/eval_jaxpr/reduce_scatter | solution.py:269
  659.7 98.4 %reduce-scatter.16.cloned.1.call-done = f32[384,768]{1,0:T(8,128)} async-done(((f32[3072,768]{1,0:T(8,128)}), f32[384,768]{1,0:T(8,128)}) %reduce-scatter.16.cloned.1.call-update) | async-done | bytes 1179664 | tf_op jit(solution)/shard_map/while/body/eval_jaxpr/reduce_scatter | solution.py:271
  774.4 26.6 %all-reduce.19 = (bf16[4608]{0:T(1024)(128)(2,1)S(1)}, bf16[768]{0:T(1024)(128)(2,1)S(1)}, bf16[768]{0:T(1024)(128)(2,1)S(1)}, bf16[768]{0:T(1024)(128)(2,1)S(1)}) all-reduce(bf16[4608]{0:T(1024)(128)(2,1)S(1)} %dynamic-update-slice.36, bf16[768]{0:T(1024)(128)(2,1)S(1)} %dynamic-update-slice.37, ...), channel_id=1, replica_groups=mesh['rep'=4,'shard'=8] {'shard'}, use_global_device_ids=true, to_apply=%add.1 | all-reduce | flops 6912 | bytes 27648 | tf_op jit(solution)/shard_map/while
  802.2 13.3 all-gather.3
  895.5 13.5 fusion.265
  927.6 16.3 %multiply_convert_fusion.12 = (bf16[1024,3072]{1,0:T(8,128)(2,1)}, f32[1024,3072]{1,0:T(8,128)}) fusion(f32[3072]{0:T(1024)S(1)} %bitcast.295, bf16[768,3072]{1,0:T(8,128)(2,1)} %all-gather.16.cloned.1.call-done, f32[1024,768]{0,1:T(8,128)} %copy-done.6, f32[768]{0:T(1024)S(1)} %get-tuple-element.1086, f32[768]{0:T(1024)S(1)} %get-tuple-element.1087, ...), kind=kOutput, calls=%fused_computation.27.clone.1 | convolution fusion | flops 4868014080 | bytes 26768384 | tf_op jit(solution)/shard_map/while/body/eval_jaxpr/dot_general | solution.py:165
  954.4 17.4 %convert_reduce_fusion.9 = (f32[3072]{0:T(1024)}, bf16[1024,3072]{1,0:T(8,128)(2,1)S(1)}) fusion(f32[1024,3072]{1,0:T(8,128)} %get-tuple-element.1090, f32[3072]{0:T(1024)S(1)} %bitcast.296, bf16[3072,768]{1,0:T(8,128)(2,1)} %all-gather.18.cloned.1.call-done, bf16[1,1,1024,768]{2,3,1,0:T(8,128)(2,1)S(1)} %copy-done.19, f32[768]{0:T(1024)S(1)} %copy-done.69), kind=kOutput, calls=%fused_computation.28.clone.1 | convolution fusion | flops 4906546176 | bytes 25193472 | tf_op jit(solution)/shard_map/while/body/eval_jaxpr/td,fd->tf/dot_general | solution.py:180
  992.7 21.4 %multiply_reduce_fusion.13 = (f32[12,512]{1,0:T(8,128)S(1)}, f32[12,512,1024]{2,1,0:T(8,128)}) fusion(f32[12,512]{1,0:T(8,128)S(1)} %log_add_fusion.5, f32[12,512,1024]{2,1,0:T(8,128)} %get-tuple-element.1084, pred[512,1024]{1,0:T(8,128)(4,1)S(1)} %copy-done.16, bf16[512,12,64]{0,2,1:T(8,128)(2,1)S(1)} %bitcast.288, ...), kind=kOutput, calls=%fused_computation.4.clone.1 | convolution fusion | flops 836757504 | bytes 53264384 | tf_op jit(solution)/shard_map/while/body/eval_jaxpr/while/body/eval_jaxpr/qhd,khd->hqk/dot_general | solution.py:116
  1014.0 17.6 %multiply_convert_fusion.14 = bf16[12,512,1024]{2,1,0:T(8,128)(2,1)S(1)} fusion(f32[12,512,1024]{2,1,0:T(8,128)} %get-tuple-element.1099, f32[12,512]{1,0:T(8,128)S(1)} %get-tuple-element.1100, f32[12,512]{1,0:T(8,128)S(1)} %log_add_fusion.5, f32[12,512,1024]{2,1,0:T(8,128)} %get-tuple-element.1084, pred[512,1024]{1,0:T(8,128)(4,1)} %get-tuple-element.1081), kind=kLoop, calls=%fused_computation.3.clone.1 | loop fusion | flops 37748736 | bytes 63488000 | tf_op jit(solution)/shard_map/while/body/eval_jaxpr/while/body/eval_jaxpr/convert_element_type | solution.py:120
  1056.4 17.8 %multiply_reduce_fusion.14 = (f32[12,512]{1,0:T(8,128)S(1)}, f32[12,512,1024]{2,1,0:T(8,128)}) fusion(f32[12,512]{1,0:T(8,128)S(1)} %log_add_fusion.4, f32[12,512,1024]{2,1,0:T(8,128)} %get-tuple-element.1080, pred[512,1024]{1,0:T(8,128)(4,1)S(1)} %copy-done.15, bf16[512,12,64]{0,2,1:T(8,128)(2,1)} %bitcast.290, bf16[1024,12,64]{0,2,1:T(8,128)(2,1)S(1)} %bitcast.280), kind=kOutput, calls=%fused_computation.1.clone.1 | convolution fusion | flops 836757504 | bytes 53264384 | tf_op jit(solution)/shard_map/while/body/eval_jaxpr/while/body/eval_jaxpr/qhd,khd->hqk/dot_general | solution.py:116
  1074.1 13.9 add_convert_fusion.9
  1088.1 17.2 %multiply_convert_fusion.15 = bf16[12,512,1024]{2,1,0:T(8,128)(2,1)S(1)} fusion(f32[12,512,1024]{2,1,0:T(8,128)} %get-tuple-element.1101, f32[12,512]{1,0:T(8,128)S(1)} %get-tuple-element.1102, f32[12,512]{1,0:T(8,128)S(1)} %log_add_fusion.4, f32[12,512,1024]{2,1,0:T(8,128)} %get-tuple-element.1080, pred[512,1024]{1,0:T(8,128)(4,1)} %get-tuple-element.1076), kind=kLoop, calls=%fused_computation.clone.1 | loop fusion | flops 37748736 | bytes 63488000 | tf_op jit(solution)/shard_map/while/body/eval_jaxpr/while/body/eval_jaxpr/convert_element_type | solution.py:120
  1133.1 14.4 fusion.282
  1196.1 28.5 %all-reduce.20 = (f32[768]{0:T(1024)}, f32[768]{0:T(1024)}, f32[3072]{0:T(1024)}, f32[768]{0:T(1024)}, f32[4608]{0:T(1024)}) all-reduce(f32[768]{0:T(1024)S(1)} %get-tuple-element.1104, f32[768]{0:T(1024)S(1)} %copy-done.62, f32[3072]{0:T(1024)S(1)} %copy-done.64, ...), channel_id=2, replica_groups=mesh['rep'=4,'shard'=8] {'shard'}, use_global_device_ids=true, to_apply=%region_16.16.clone | all-reduce | flops 9984 | bytes 79872 | tf_op jit(solution)/shard_map/while
  1233.9 71.2 %reduce-scatter.10.cloned.1.call-done = f32[96,2304]{1,0:T(8,128)} async-done(((f32[768,2304]{1,0:T(8,128)}), f32[96,2304]{1,0:T(8,128)}) %reduce-scatter.10.cloned.1.call-update) | async-done | bytes 884752 | tf_op jit(solution)/shard_map/while/body/eval_jaxpr/reduce_scatter | solution.py:266
  1306.5 98.8 %reduce-scatter.14.cloned.1.call-done = f32[96,3072]{1,0:T(8,128)} async-done(((f32[768,3072]{1,0:T(8,128)}), f32[96,3072]{1,0:T(8,128)}) %reduce-scatter.14.cloned.1.call-update) | async-done | bytes 1179664 | tf_op jit(solution)/shard_map/while/body/eval_jaxpr/reduce_scatter | solution.py:269
  1407.1 98.4 %reduce-scatter.16.cloned.1.call-done = f32[384,768]{1,0:T(8,128)} async-done(((f32[3072,768]{1,0:T(8,128)}), f32[384,768]{1,0:T(8,128)}) %reduce-scatter.16.cloned.1.call-update) | async-done | bytes 1179664 | tf_op jit(solution)/shard_map/while/body/eval_jaxpr/reduce_scatter | solution.py:271
  1531.7 52.0 %all-reduce.23.cloned.1.call-done = (bf16[96,2304]{1,0:T(8,128)(2,1)}, bf16[96,768]{1,0:T(8,128)(2,1)}, bf16[96,3072]{1,0:T(8,128)(2,1)}, bf16[384,768]{1,0:T(8,128)(2,1)}, bf16[128,576]{0,1:T(8,128)(2,1)}) async-done(((bf16[96,2304]{1,0:T(8,128)(2,1)}, bf16[96,768]{1,0:T(8,128)(2,1)}, bf16[96,3072]{1,0:T(8,128)(2,1)}, bf16[384,768]{1,0:T(8,128)(2,1)}, bf16[128,576]{0,1:T(8,128)(2,1)}), ...) | async-done | bytes 1916944 | tf_op jit(solution)/shard_map/psum | solution.py:282
  (653 shorter events, 542.7 us)
Async XLA Ops:
  8.4 67.7 %all-gather.14.cloned.1.call-start = ((), (), s32[]{:S(2)}) async-start(), calls=%async_computation.8 | async-start | bytes 1327104 | tf_op jit(solution)/shard_map/while/body/eval_jaxpr/all_gather | solution.py:257
  9.1 70.4 %all-gather.10.cloned.1.call-start = ((), (), s32[]{:S(2)}) async-start(), calls=%async_computation.6 | async-start | bytes 3981312 | tf_op jit(solution)/shard_map/while/body/eval_jaxpr/all_gather | solution.py:250
  9.8 163.1 %all-gather.12.cloned.1.call-start = ((), (), s32[]{:S(2)}) async-start(), calls=%async_computation.7 | async-start | bytes 1327104 | tf_op jit(solution)/shard_map/while/body/eval_jaxpr/all_gather | solution.py:251
  10.6 169.3 %all-gather.16.cloned.1.call-start = ((), (), s32[]{:S(2)}) async-start(), calls=%async_computation.9 | async-start | bytes 5308416 | tf_op jit(solution)/shard_map/while/body/eval_jaxpr/all_gather | solution.py:253
  11.2 195.5 %all-gather.18.cloned.1.call-start = ((), (), s32[]{:S(2)}) async-start(), calls=%async_computation.10 | async-start | bytes 5308416 | tf_op jit(solution)/shard_map/while/body/eval_jaxpr/all_gather | solution.py:255
  11.7 470.3 %reduce-scatter.18.cloned.1.call-start = ((), (), s32[]{:S(2)}) async-start(), calls=%async_computation.15 | async-start | bytes 2654208 | tf_op jit(solution)/shard_map/while
  404.6 78.5 %reduce-scatter.12.cloned.1.call-start = ((), (), s32[]{:S(2)}) async-start(), calls=%async_computation.12 | async-start | bytes 2654208 | tf_op jit(solution)/shard_map/while/body/eval_jaxpr/reduce_scatter | solution.py:267
  409.6 148.2 %reduce-scatter.10.cloned.1.call-start = ((), (), s32[]{:S(2)}) async-start(), calls=%async_computation.11 | async-start | bytes 7962624 | tf_op jit(solution)/shard_map/while/body/eval_jaxpr/reduce_scatter | solution.py:266
  418.8 239.2 %reduce-scatter.14.cloned.1.call-start = ((), (), s32[]{:S(2)}) async-start(), calls=%async_computation.13 | async-start | bytes 10616832 | tf_op jit(solution)/shard_map/while/body/eval_jaxpr/reduce_scatter | solution.py:269
  431.3 326.7 %reduce-scatter.16.cloned.1.call-start = ((), (), s32[]{:S(2)}) async-start(), calls=%async_computation.14 | async-start | bytes 10616832 | tf_op jit(solution)/shard_map/while/body/eval_jaxpr/reduce_scatter | solution.py:271
  478.7 179.3 %copy-start.33 = (f32[96,3072]{1,0:T(8,128)S(1)}, f32[96,3072]{1,0:T(8,128)}, u32[]{:S(2)}) copy-start(f32[96,3072]{1,0:T(8,128)} %get-tuple-element.1174) | copy-start | bytes 3538948 | tf_op jit(solution)/shard_map/while
  479.6 180.0 %copy-start.78 = (f32[96]{0:T(128)}, f32[96]{0:T(128)S(1)}, u32[]{:S(2)}) copy-start(f32[96]{0:T(128)S(1)} %fusion.288) | copy-start | bytes 1156 | tf_op jit(solution)/shard_map/while
  480.4 179.2 %copy-start.81 = (f32[96]{0:T(128)}, f32[96]{0:T(128)S(1)}, u32[]{:S(2)}) copy-start(f32[96]{0:T(128)S(1)} %get-tuple-element.1212) | copy-start | bytes 1156 | tf_op jit(solution)/shard_map/while
  481.2 178.4 %copy-start.75 = (f32[384]{0:T(512)}, f32[384]{0:T(512)S(1)}, u32[]{:S(2)}) copy-start(f32[384]{0:T(512)S(1)} %dynamic-slice_add_fusion.4) | copy-start | bytes 4612 | tf_op jit(solution)/shard_map/while
  485.0 273.0 %copy-start.30 = (f32[384,768]{1,0:T(8,128)S(1)}, f32[384,768]{1,0:T(8,128)}, u32[]{:S(2)}) copy-start(f32[384,768]{1,0:T(8,128)} %get-tuple-element.1176) | copy-start | bytes 3538948 | tf_op jit(solution)/shard_map/while
  559.1 200.5 %copy-start.39 = (f32[96,2304]{1,0:T(8,128)}, f32[96,2304]{1,0:T(8,128)S(1)}, u32[]{:S(2)}) copy-start(f32[96,2304]{1,0:T(8,128)S(1)} %select_add_fusion.10) | copy-start | bytes 2654212 | tf_op jit(solution)/shard_map/while
  760.8 63.1 %all-gather.14.cloned.1.call-start = ((), (), s32[]{:S(2)}) async-start(), calls=%async_computation.8 | async-start | bytes 1327104 | tf_op jit(solution)/shard_map/while/body/eval_jaxpr/all_gather | solution.py:257
  761.5 65.7 %all-gather.10.cloned.1.call-start = ((), (), s32[]{:S(2)}) async-start(), calls=%async_computation.6 | async-start | bytes 3981312 | tf_op jit(solution)/shard_map/while/body/eval_jaxpr/all_gather | solution.py:250
  762.1 158.4 %all-gather.12.cloned.1.call-start = ((), (), s32[]{:S(2)}) async-start(), calls=%async_computation.7 | async-start | bytes 1327104 | tf_op jit(solution)/shard_map/while/body/eval_jaxpr/all_gather | solution.py:251
  762.9 164.7 %all-gather.16.cloned.1.call-start = ((), (), s32[]{:S(2)}) async-start(), calls=%async_computation.9 | async-start | bytes 5308416 | tf_op jit(solution)/shard_map/while/body/eval_jaxpr/all_gather | solution.py:253
  763.5 191.0 %all-gather.18.cloned.1.call-start = ((), (), s32[]{:S(2)}) async-start(), calls=%async_computation.10 | async-start | bytes 5308416 | tf_op jit(solution)/shard_map/while/body/eval_jaxpr/all_gather | solution.py:255
  764.0 465.8 %reduce-scatter.18.cloned.1.call-start = ((), (), s32[]{:S(2)}) async-start(), calls=%async_computation.15 | async-start | bytes 2654208 | tf_op jit(solution)/shard_map/while
  1152.4 78.6 %reduce-scatter.12.cloned.1.call-start = ((), (), s32[]{:S(2)}) async-start(), calls=%async_computation.12 | async-start | bytes 2654208 | tf_op jit(solution)/shard_map/while/body/eval_jaxpr/reduce_scatter | solution.py:267
  1157.3 147.8 %reduce-scatter.10.cloned.1.call-start = ((), (), s32[]{:S(2)}) async-start(), calls=%async_computation.11 | async-start | bytes 7962624 | tf_op jit(solution)/shard_map/while/body/eval_jaxpr/reduce_scatter | solution.py:266
  1166.5 238.8 %reduce-scatter.14.cloned.1.call-start = ((), (), s32[]{:S(2)}) async-start(), calls=%async_computation.13 | async-start | bytes 10616832 | tf_op jit(solution)/shard_map/while/body/eval_jaxpr/reduce_scatter | solution.py:269
  1179.1 326.3 %reduce-scatter.16.cloned.1.call-start = ((), (), s32[]{:S(2)}) async-start(), calls=%async_computation.14 | async-start | bytes 10616832 | tf_op jit(solution)/shard_map/while/body/eval_jaxpr/reduce_scatter | solution.py:271
  1226.5 178.8 %copy-start.33 = (f32[96,3072]{1,0:T(8,128)S(1)}, f32[96,3072]{1,0:T(8,128)}, u32[]{:S(2)}) copy-start(f32[96,3072]{1,0:T(8,128)} %get-tuple-element.1174) | copy-start | bytes 3538948 | tf_op jit(solution)/shard_map/while
  1227.4 179.6 %copy-start.78 = (f32[96]{0:T(128)}, f32[96]{0:T(128)S(1)}, u32[]{:S(2)}) copy-start(f32[96]{0:T(128)S(1)} %fusion.288) | copy-start | bytes 1156 | tf_op jit(solution)/shard_map/while
  1228.2 178.8 %copy-start.81 = (f32[96]{0:T(128)}, f32[96]{0:T(128)S(1)}, u32[]{:S(2)}) copy-start(f32[96]{0:T(128)S(1)} %get-tuple-element.1212) | copy-start | bytes 1156 | tf_op jit(solution)/shard_map/while
  1233.9 271.5 %copy-start.30 = (f32[384,768]{1,0:T(8,128)S(1)}, f32[384,768]{1,0:T(8,128)}, u32[]{:S(2)}) copy-start(f32[384,768]{1,0:T(8,128)} %get-tuple-element.1176) | copy-start | bytes 3538948 | tf_op jit(solution)/shard_map/while
  1306.5 200.5 %copy-start.39 = (f32[96,2304]{1,0:T(8,128)}, f32[96,2304]{1,0:T(8,128)S(1)}, u32[]{:S(2)}) copy-start(f32[96,2304]{1,0:T(8,128)S(1)} %select_add_fusion.10) | copy-start | bytes 2654212 | tf_op jit(solution)/shard_map/while
  1509.7 74.0 %all-reduce.23.cloned.1.call-start = ((), (), s32[]{:S(2)}) async-start(), calls=%async_computation.5 | async-start | bytes 3833856 | tf_op jit(solution)/shard_map/psum | solution.py:282
  (168 other events, 3298.9 us)
Sparse Core Ops, SparseCore 0:
  10.8 25.5 all-gather.13
  38.1 41.3 all-gather.9
  81.1 21.6 all-gather.11
  104.3 50.8 all-gather.15
  156.6 49.9 all-gather.17
  404.7 35.7 reduce-scatter.17
  442.9 36.0 reduce-scatter.11
  481.3 76.3 reduce-scatter.9
  560.0 97.8 reduce-scatter.13
  660.1 97.8 reduce-scatter.15
  763.3 21.2 all-gather.13
  786.1 41.0 all-gather.9
  828.9 21.6 all-gather.11
  852.0 50.8 all-gather.15
  904.4 49.9 all-gather.17
  1152.5 35.7 reduce-scatter.17
  1190.5 36.0 reduce-scatter.11
  1228.7 76.3 reduce-scatter.9
  1307.4 97.8 reduce-scatter.13
  1407.5 97.8 reduce-scatter.15
Sparse Core Ops, SparseCore 1:
  1518.4 65.2 all-reduce.22
where the time goes:
time: 1600 us
  waiting for transfers between devices  619 us (39%)
  matrix products  484 us (30%)
  other arithmetic  203 us (13%)
  blocking collectives  152 us (10%)
  local copies, waits for them, and re-layouts  115 us (7%)
    reduce_scatter x2, waiting for transfers between devices, micro_batch(): lax.psum_scatter(full_grads[4], 'shard', scatter_dimension=0, tiled=True)  198 us
    reduce_scatter x2, waiting for transfers between devices, micro_batch(): lax.psum_scatter(full_grads[6], 'shard', scatter_dimension=0, tiled=True)  197 us
    reduce_scatter x2, waiting for transfers between devices, micro_batch(): lax.psum_scatter(full_grads[1], 'shard', scatter_dimension=0, tiled=True)  144 us
    while x4, blocking collectives  115 us
    dot_general x4, matrix products, attention_backward(): jnp.einsum('qhd,khd->hqk', block_d, values_all, preferred_element_type=jn...  78.2 us
    convert_element_type x4, other arithmetic, attention_backward(): d_scores = (probs_full * (d_probs - inner_sum)).astype(jnp.bfloat16)  69.6 us
    while x378, local copies, waits for them, and re-layouts  55.1 us
    dot_general x4, matrix products, attention_backward(): jnp.einsum('hqk,qhd->khd', probs_low, block_d, preferred_element_type=jnp...  54.2 us
  transfers between devices with their start and end apart: 21, of which 11 were waited for; matrix products, arithmetic and copies ran while one was open for 23% of the time, Pallas kernels for 0%

commit v1 on v0

v1 whole, which is shorter than its diff:
```python
import functools
import math

import jax
import jax.numpy as jnp
from jax import lax
from jax.experimental import pallas as pl
from jax.experimental.pallas import tpu as pltpu
from jax.sharding import PartitionSpec as P

D=768; HEADS=12; HD=64; TLEN=1024; TRUNK=256
NT=(((1,),(1,)),((),()))
TN=(((0,),(0,)),((),()))
BIG=-1e30
F32=jnp.float32; BF=jnp.bfloat16

def seg_tables(len_ref, tree, rows, lanes=128):
    pos = lax.broadcasted_iota(jnp.int32,(rows,lanes),0) - TRUNK
    lane = lax.broadcasted_iota(jnp.int32,(rows,lanes),1)
    seg = jnp.where(pos>=0,1,0)
    bound = jnp.int32(0)
    for j in range(12):
        bound = bound + len_ref[tree, j]
        seg = seg + jnp.where((pos>=bound),1,0)
    parent = jnp.where(seg>=5, 1+lax.shift_right_arithmetic(seg-5,1), 0)
    ok = (lane==0)|(lane==seg)|(lane==parent)|(lane>12)
    a = jnp.where(ok, 0.0, BIG).astype(BF)
    b = jnp.where(lane==seg, 1.0, 0.0).astype(BF)
    return a,b

def fwd_kernel(len_ref, q_ref,k_ref,v_ref,o_ref,lse_ref,a_s,kaug,vaug):
    t=pl.program_id(0); hp=pl.program_id(1)
    @pl.when(hp==0)
    def _():
        a,b=seg_tables(len_ref,t,TLEN)
        a_s[...]=a
        kaug[:,128:]=b
        vaug[:,128:]=jnp.ones((TLEN,128),BF)
        lse_ref[...]=jnp.zeros_like(lse_ref)
    kaug[:,:128]=k_ref[...]
    vaug[:,:128]=v_ref[...]
    lane=lax.broadcasted_iota(jnp.int32,(256,128),1)
    for qt in range(4):
        rows=slice(qt*256,qt*256+256)
        nk=256 if qt==0 else TLEN
        q2=q_ref[rows,:]
        outs=[]
        lse_acc=lse_ref[rows,:]
        for h in range(2):
            keep=(lane<64) if h==0 else (lane>=64)
            qh=(jnp.where(keep,q2.astype(F32),0.0)*0.125).astype(BF)
            qa=jnp.concatenate([qh,a_s[rows,:]],axis=1)
            s=lax.dot_general(qa,kaug[:nk,:],NT,preferred_element_type=F32)
            m=jnp.max(s,axis=1,keepdims=True)
            p=jnp.exp(s-m).astype(BF)
            o=jnp.dot(p,vaug[:nk,:],preferred_element_type=F32)
            l=o[:,128:]
            outs.append(o[:,:128]/l)
            lse_acc=jnp.where(lane==2*hp+h, m+jnp.log(l), lse_acc)
        lse_ref[rows,:]=lse_acc
        o_ref[rows,:]=jnp.where(lane<64,outs[0],outs[1]).astype(BF)

def attn_fwd(qkv, lens, trees=2):
    gs=pltpu.PrefetchScalarGridSpec(num_scalar_prefetch=1,grid=(trees,6),
      in_specs=[pl.BlockSpec((TLEN,128),lambda t,h,L:(t,h)),
                pl.BlockSpec((TLEN,128),lambda t,h,L:(t,6+h)),
                pl.BlockSpec((TLEN,128),lambda t,h,L:(t,12+h))],
      out_specs=[pl.BlockSpec((TLEN,128),lambda t,h,L:(t,h)),
                 pl.BlockSpec((TLEN,128),lambda t,h,L:(t,0))],
      scratch_shapes=[pltpu.VMEM((TLEN,128),BF),pltpu.VMEM((TLEN,256),BF),pltpu.VMEM((TLEN,256),BF)])
    return pl.pallas_call(fwd_kernel,grid_spec=gs,
      out_shape=[jax.ShapeDtypeStruct((trees*TLEN,D),BF),jax.ShapeDtypeStruct((trees*TLEN,128),F32)],
      compiler_params=pltpu.CompilerParams(vmem_limit_bytes=60<<20),name="attn_fwd")(lens,qkv,qkv,qkv)


def split3(x):
    hi=x.astype(BF).astype(F32); r=x-hi
    mid=r.astype(BF).astype(F32)
    return hi,mid,r-mid

def bwd_kernel(mode, len_ref,q_ref,k_ref,v_ref,do_ref,o_ref,lse_ref,dq_ref,dk_ref,dv_ref,a_s,b_s,ka,va,dk_acc,dv_acc):
    t=pl.program_id(0); hp=pl.program_id(1)
    lane=lax.broadcasted_iota(jnp.int32,(256,128),1)
    laneT=lax.broadcasted_iota(jnp.int32,(TLEN,128),1)
    @pl.when(hp==0)
    def _():
        a,b=seg_tables(len_ref,t,TLEN)
        hi,mid,lo=split3(lse_ref[...])
        ext=pltpu.roll(hi,16,1)+pltpu.roll(mid,32,1)+pltpu.roll(lo,48,1)
        a_s[...]=(a.astype(F32)-ext).astype(BF)
        b_s[...]=b
        va[:,128:]=jnp.where(laneT<3,1.0,0.0).astype(BF)
    ka[:,:128]=k_ref[...]
    va[:,:128]=v_ref[...]
    kf=k_ref[...].astype(F32)*0.125
    for h in range(2):
        hd=2*hp+h
        on=(laneT==16+hd)|(laneT==32+hd)|(laneT==48+hd)
        ka[:,128:]=jnp.where(on,1.0,b_s[...].astype(F32)).astype(BF)
        keep=(lane<64) if h==0 else (lane>=64)
        keepT=(laneT<64) if h==0 else (laneT>=64)
        kh=jnp.where(keepT,kf,0.0).astype(BF)
        for qt in range(4):
            rows=slice(qt*256,qt*256+256)
            nk=256 if qt==0 else TLEN
            qm=(jnp.where(keep,q_ref[rows,:].astype(F32),0.0)*0.125).astype(BF)
            dof=jnp.where(keep,do_ref[rows,:].astype(F32),0.0)
            dom=dof.astype(BF)
            delta=jnp.sum(dof*o_ref[rows,:].astype(F32),axis=1,keepdims=True)
            dhi,dmid,dlo=split3(delta)
            ext=jnp.where(lane==0,dhi,jnp.where(lane==1,dmid,jnp.where(lane==2,dlo,0.0)))
            doa=jnp.concatenate([dom,(-ext).astype(BF)],axis=1)
            qa=jnp.concatenate([qm,a_s[rows,:]],axis=1)
            st=lax.dot_general(ka[:nk,:],qa,NT,preferred_element_type=F32)
            dpt=lax.dot_general(va[:nk,:],doa,NT,preferred_element_type=F32)
            pt=jnp.exp(st)
            plow=pt.astype(BF)
            ds=(pt*dpt).astype(BF)
            dvp=jnp.dot(plow,dom,preferred_element_type=F32)
            dkp=jnp.dot(ds,qm,preferred_element_type=F32)
            if h==0 and qt==0:
                dk_acc[...]=jnp.zeros_like(dk_acc); dv_acc[...]=jnp.zeros_like(dv_acc)
            dv_acc[:nk,:]+=dvp
            dk_acc[:nk,:]+=dkp
            if mode=="tn":
                dq=lax.dot_general(ds,kh[:nk,:],TN,preferred_element_type=F32)
            else:
                dqt=lax.dot_general(kh[:nk,:],ds,TN,preferred_element_type=F32)
                dq=dqt.T
            if h==0: dq_ref[rows,:]=dq.astype(BF)
            else: dq_ref[rows,:]=jnp.where(lane<64,dq_ref[rows,:].astype(F32),dq).astype(BF)
    dk_ref[...]=dk_acc[...].astype(BF)
    dv_ref[...]=dv_acc[...].astype(BF)

def attn_bwd(qkv, lens, do, o, lse, trees=2, mode="nt"):
    b=lambda off: pl.BlockSpec((TLEN,128),lambda t,h,L:(t,off+h))
    gs=pltpu.PrefetchScalarGridSpec(num_scalar_prefetch=1,grid=(trees,6),
      in_specs=[b(0),b(6),b(12),b(0),b(0),pl.BlockSpec((TLEN,128),lambda t,h,L:(t,0))],
      out_specs=[b(0),b(0),b(0)],
      scratch_shapes=[pltpu.VMEM((TLEN,128),BF),pltpu.VMEM((TLEN,128),BF),pltpu.VMEM((TLEN,256),BF),pltpu.VMEM((TLEN,256),BF),
                      pltpu.VMEM((TLEN,128),F32),pltpu.VMEM((TLEN,128),F32)])
    o1=jax.ShapeDtypeStruct((trees*TLEN,D),BF)
    return pl.pallas_call(functools.partial(bwd_kernel,mode),grid_spec=gs,out_shape=[o1,o1,o1],
      compiler_params=pltpu.CompilerParams(vmem_limit_bytes=60<<20),name="attn_bwd")(lens,qkv,qkv,qkv,do,o,lse)
FF=3072
VL=63<<20
def norm_parts(x):
    mean=jnp.mean(x,axis=1,keepdims=True)
    cen=x-mean
    var=jnp.mean(cen*cen,axis=1,keepdims=True)
    rs=lax.rsqrt(var+1e-5)
    return cen*rs, rs

def qkv_kernel(x_ref,mod_ref,gain_ref,w_ref,ha_ref,o_ref):
    xhat,_=norm_parts(x_ref[...].astype(F32))
    m=mod_ref[0]
    h=(xhat*gain_ref[...]*(1.0+m[1:2])+m[0:1]).astype(BF)
    ha_ref[...]=h
    for j in range(3):
        c=slice(j*768,(j+1)*768)
        o_ref[:,c]=jnp.dot(h,w_ref[:,c],preferred_element_type=F32).astype(BF)

def qkv_fwd(x,mod,gain,w,RB=512):
    n=x.shape[0]; per=TLEN//RB
    return pl.pallas_call(qkv_kernel,grid=(n//RB,),
      in_specs=[pl.BlockSpec((RB,D),lambda i:(i,0)),pl.BlockSpec((1,6,D),lambda i:(i//per,0,0)),
        pl.BlockSpec((1,D),lambda i:(0,0)),pl.BlockSpec((D,3*D),lambda i:(0,0),pipeline_mode=pl.Buffered(1))],
      out_specs=[pl.BlockSpec((RB,D),lambda i:(i,0)),pl.BlockSpec((RB,3*D),lambda i:(i,0))],
      out_shape=[jax.ShapeDtypeStruct((n,D),BF),jax.ShapeDtypeStruct((n,3*D),BF)],
      compiler_params=pltpu.CompilerParams(vmem_limit_bytes=VL),name="qkv_fwd")(x,mod,gain,w)

def pre_kernel(x_ref,c_ref,mx_ref,mod_ref,gain_ref,w_ref,br_ref,hm_ref,dd_ref):
    m=mod_ref[0]
    br=jnp.dot(mx_ref[...],w_ref[...],preferred_element_type=F32)
    br_ref[...]=br
    mid=x_ref[...].astype(F32)+m[2:3]*br
    xhat,_=norm_parts(mid)
    hm_ref[...]=(xhat*gain_ref[...]*(1.0+m[4:5])+m[3:4]).astype(BF)
    dd_ref[...]=(c_ref[...].astype(F32)*m[5:6]).astype(BF)

def mlp_pre(x,c,mixed,mod,gain,w,RB=512):
    n=x.shape[0]; per=TLEN//RB
    rb=pl.BlockSpec((RB,D),lambda i:(i,0))
    return pl.pallas_call(pre_kernel,grid=(n//RB,),
      in_specs=[rb,rb,rb,pl.BlockSpec((1,6,D),lambda i:(i//per,0,0)),
        pl.BlockSpec((1,D),lambda i:(0,0)),pl.BlockSpec((D,D),lambda i:(0,0),pipeline_mode=pl.Buffered(1))],
      out_specs=[rb,rb,rb],
      out_shape=[jax.ShapeDtypeStruct((n,D),F32),jax.ShapeDtypeStruct((n,D),BF),jax.ShapeDtypeStruct((n,D),BF)],
      compiler_params=pltpu.CompilerParams(vmem_limit_bytes=VL),name="mlp_pre")(x,c,mixed,mod,gain,w)

C0=math.sqrt(2/math.pi); C1=0.044715
def core_kernel(RB,hm_ref,dd_ref,wu_ref,bu_ref,wd_ref,dn_ref,dh_ref,gu_ref,gb_ref,gd_ref,act_s,dup_s):
    j=pl.program_id(0)
    n=hm_ref.shape[0]
    @pl.when(j==0)
    def _():
        dn_ref[...]=jnp.zeros_like(dn_ref); dh_ref[...]=jnp.zeros_like(dh_ref)
    gb=jnp.zeros((1,wu_ref.shape[1]),F32)
    for r in range(n//RB):
        rows=slice(r*RB,(r+1)*RB)
        u=jnp.dot(hm_ref[rows,:],wu_ref[...],preferred_element_type=F32)+bu_ref[...]
        u2=u*u
        th=jnp.tanh(C0*u*(1.0+C1*u2))
        cdf=0.5+0.5*th
        act=(u*cdf).astype(BF)
        act_s[rows,:]=act
        gp=cdf+(0.5*C0)*u*(1.0-th*th)*(1.0+(3*C1)*u2)
        da=lax.dot_general(dd_ref[rows,:],wd_ref[...],NT,preferred_element_type=F32)
        dup=(da*gp).astype(BF)
        dup_s[rows,:]=dup
        gb=gb+jnp.sum(dup.astype(F32),axis=0,keepdims=True)
        dn_ref[rows,:]+=jnp.dot(act,wd_ref[...],preferred_element_type=F32)
        dh_ref[rows,:]+=lax.dot_general(dup,wu_ref[...],NT,preferred_element_type=F32)
    gb_ref[...]=gb
    gu_ref[...]=lax.dot_general(hm_ref[...],dup_s[...],TN,preferred_element_type=F32).astype(BF)
    gd_ref[...]=lax.dot_general(act_s[...],dd_ref[...],TN,preferred_element_type=F32).astype(BF)

def mlp_core(hm,dd,wu,bu,wd,C=512,RB=256):
    n=hm.shape[0]
    full=pl.BlockSpec((n,D),lambda j:(0,0),pipeline_mode=pl.Buffered(1))
    return pl.pallas_call(functools.partial(core_kernel,RB),grid=(FF//C,),
      in_specs=[full,full,pl.BlockSpec((D,C),lambda j:(0,j)),pl.BlockSpec((1,C),lambda j:(0,j)),pl.BlockSpec((C,D),lambda j:(j,0))],
      out_specs=[pl.BlockSpec((n,D),lambda j:(0,0)),pl.BlockSpec((n,D),lambda j:(0,0)),
        pl.BlockSpec((D,C),lambda j:(0,j)),pl.BlockSpec((1,C),lambda j:(0,j)),pl.BlockSpec((C,D),lambda j:(j,0))],
      out_shape=[jax.ShapeDtypeStruct((n,D),F32),jax.ShapeDtypeStruct((n,D),F32),jax.ShapeDtypeStruct((D,FF),BF),
        jax.ShapeDtypeStruct((1,FF),F32),jax.ShapeDtypeStruct((FF,D),BF)],
      scratch_shapes=[pltpu.VMEM((n,C),BF),pltpu.VMEM((n,C),BF)],
      compiler_params=pltpu.CompilerParams(vmem_limit_bytes=VL),name="mlp_core")(hm,dd,wu,bu,wd)

def rsum(x): return jnp.sum(x,axis=0,keepdims=True)

def post_kernel(per,x_ref,c_ref,mx_ref,br_ref,dn_ref,dh_ref,dd_ref,mod_ref,gain_ref,bd_ref,w_ref,
                out_ref,dmid_ref,dmx_ref,st_ref,gw_ref,acc):
    i=pl.program_id(0); last=pl.num_programs(0)-1
    m=mod_ref[0]
    c=c_ref[...].astype(F32)
    br=br_ref[...]
    mid=x_ref[...].astype(F32)+m[2:3]*br
    down=dn_ref[...]+bd_ref[...]
    out_ref[...]=(mid+m[5:6]*down).astype(BF)
    xhat,rs=norm_parts(mid)
    dh=dh_ref[...]
    gain=gain_ref[...]
    dhx=dh*xhat
    sdh=rsum(dh); sdhx=rsum(dhx)
    e=dh*((1.0+m[4:5])*gain)
    me=jnp.mean(e,axis=1,keepdims=True)
    mex=jnp.mean(e*xhat,axis=1,keepdims=True)
    dmid=c+(e-me-xhat*mex)*rs
    dmid_ref[...]=dmid
    dbr=(dmid*m[2:3]).astype(BF)
    dmx_ref[...]=lax.dot_general(dbr,w_ref[...],NT,preferred_element_type=F32).astype(BF)
    stats=jnp.concatenate([rsum(dmid*br),sdh,sdhx*gain,rsum(c*down),sdhx*(1.0+m[4:5]),rsum(dd_ref[...].astype(F32)),
                           jnp.zeros((2,D),F32)],axis=0)
    @pl.when(lax.rem(i,per)==0)
    def _(): st_ref[0]=stats
    @pl.when(lax.rem(i,per)!=0)
    def _(): st_ref[0]+=stats
    g=lax.dot_general(mx_ref[...],dbr,TN,preferred_element_type=F32)
    @pl.when(i==0)
    def _(): acc[...]=g
    @pl.when(i!=0)
    def _(): acc[...]+=g
    @pl.when(i==last)
    def _(): gw_ref[...]=acc[...].astype(BF)

def mlp_post(x,c,mixed,br,dn,dh,dd,mod,gain,bd,w,RB=256):
    n=x.shape[0]; per=TLEN//RB
    rb=pl.BlockSpec((RB,D),lambda i:(i,0)); vec=pl.BlockSpec((1,D),lambda i:(0,0))
    return pl.pallas_call(functools.partial(post_kernel,per),grid=(n//RB,),
      in_specs=[rb]*7+[pl.BlockSpec((1,6,D),lambda i:(i//per,0,0)),vec,vec,pl.BlockSpec((D,D),lambda i:(0,0),pipeline_mode=pl.Buffered(1))],
      out_specs=[rb,rb,rb,pl.BlockSpec((1,8,D),lambda i:(i//per,0,0)),pl.BlockSpec((D,D),lambda i:(0,0))],
      out_shape=[jax.ShapeDtypeStruct((n,D),BF),jax.ShapeDtypeStruct((n,D),F32),jax.ShapeDtypeStruct((n,D),BF),
        jax.ShapeDtypeStruct((n//TLEN,8,D),F32),jax.ShapeDtypeStruct((D,D),BF)],
      scratch_shapes=[pltpu.VMEM((D,D),F32)],
      compiler_params=pltpu.CompilerParams(vmem_limit_bytes=VL),name="mlp_post")(x,c,mixed,br,dn,dh,dd,mod,gain,bd,w)

def qkvb_kernel(per,x_ref,ha_ref,dq_ref,dk_ref,dv_ref,dmid_ref,mod_ref,gain_ref,w_ref,dx_ref,st_ref,gw_ref,acc):
    i=pl.program_id(0); last=pl.num_programs(0)-1
    m=mod_ref[0]; gain=gain_ref[...]
    dh=None
    ha=ha_ref[...]
    for j,ref in enumerate((dq_ref,dk_ref,dv_ref)):
        c=slice(j*D,(j+1)*D)
        part=lax.dot_general(ref[...],w_ref[:,c],NT,preferred_element_type=F32)
        dh=part if dh is None else dh+part
        g=lax.dot_general(ha,ref[...],TN,preferred_element_type=F32)
        @pl.when(i==0)
        def _(): acc[:,c]=g
        @pl.when(i!=0)
        def _(): acc[:,c]+=g
    xhat,rs=norm_parts(x_ref[...].astype(F32))
    sdh=rsum(dh); sdhx=rsum(dh*xhat)
    e=dh*((1.0+m[1:2])*gain)
    me=jnp.mean(e,axis=1,keepdims=True)
    mex=jnp.mean(e*xhat,axis=1,keepdims=True)
    dx_ref[...]=(dmid_ref[...]+(e-me-xhat*mex)*rs).astype(BF)
    stats=jnp.concatenate([sdh,sdhx*gain,sdhx*(1.0+m[1:2]),jnp.zeros((5,D),F32)],axis=0)
    @pl.when(lax.rem(i,per)==0)
    def _(): st_ref[0]=stats
    @pl.when(lax.rem(i,per)!=0)
    def _(): st_ref[0]+=stats
    @pl.when(i==last)
    def _(): gw_ref[...]=acc[...].astype(BF)

def qkv_bwd(x,ha,dq,dk,dv,dmid,mod,gain,w,RB=512):
    n=x.shape[0]; per=TLEN//RB
    rb=pl.BlockSpec((RB,D),lambda i:(i,0)); vec=pl.BlockSpec((1,D),lambda i:(0,0))
    return pl.pallas_call(functools.partial(qkvb_kernel,per),grid=(n//RB,),
      in_specs=[rb]*6+[pl.BlockSpec((1,6,D),lambda i:(i//per,0,0)),vec,pl.BlockSpec((D,3*D),lambda i:(0,0),pipeline_mode=pl.Buffered(1))],
      out_specs=[rb,pl.BlockSpec((1,8,D),lambda i:(i//per,0,0)),pl.BlockSpec((D,3*D),lambda i:(0,0))],
      out_shape=[jax.ShapeDtypeStruct((n,D),BF),jax.ShapeDtypeStruct((n//TLEN,8,D),F32),jax.ShapeDtypeStruct((D,3*D),BF)],
      scratch_shapes=[pltpu.VMEM((D,3*D),F32)],
      compiler_params=pltpu.CompilerParams(vmem_limit_bytes=VL),name="qkv_bwd")(x,ha,dq,dk,dv,dmid,mod,gain,w)


HIGHEST = lax.Precision.HIGHEST
COND = 128


def time_cond(indices):
    halfway = COND // 2
    frequency = jnp.exp(-math.log(10000.0) * jnp.arange(halfway, dtype=F32) / halfway)
    angles = indices.astype(F32)[..., None] * frequency
    return jax.nn.silu(jnp.concatenate([jnp.cos(angles), jnp.sin(angles)], axis=-1))


def per_device(shards, tokens, cotangent, timestep, seg_lengths, attn_gain, w_qkv, w_out, mlp_gain,
               w_up, b_up, w_down, b_down, w_mod, b_mod):
    both = ("rep", "shard")
    trees = tokens.shape[0] * tokens.shape[1]
    x = tokens.reshape(trees * TLEN, D)
    c = cotangent.reshape(trees * TLEN, D)
    lens = seg_lengths.reshape(trees, 12)
    gather = lambda w, axis=0: lax.all_gather(w, "shard", axis=axis, tiled=True)
    small = jnp.concatenate([attn_gain, mlp_gain, b_up, b_down, b_mod])
    sizes = [v.shape[0] for v in (attn_gain, mlp_gain, b_up, b_down, b_mod)]
    smalls = gather(small[None])
    vecs, at = [], 0
    for size in sizes:
        vecs.append(smalls[:, at:at + size].reshape(1, -1).astype(F32))
        at += size
    gain_a, gain_m, up_b, down_b, mod_b = vecs
    mod_w = gather(w_mod, 1)
    cond = time_cond(timestep.reshape(trees)).astype(BF)
    mod = (jnp.dot(cond, mod_w, preferred_element_type=F32) + mod_b).reshape(trees, 6, D)
    wq = gather(w_qkv)
    wo = gather(w_out)
    wu = gather(w_up)
    wd = gather(w_down)
    ha, qkv = qkv_fwd(x, mod, gain_a, wq)
    o, lse = attn_fwd(qkv, lens, trees)
    br, hm, dd = mlp_pre(x, c, o, mod, gain_m, wo)
    dn, dh, gu, gb, gd = mlp_core(hm, dd, wu, up_b, wd)
    scatter = lambda g: lax.psum_scatter(g, "shard", scatter_dimension=0, tiled=True)
    finish = lambda g: lax.psum(g, "rep").astype(F32)
    gu = finish(scatter(gu))
    gd = finish(scatter(gd))
    out, dmid, dmx, st, go = mlp_post(x, c, o, br, dn, dh, dd, mod, gain_m, down_b, wo)
    go = finish(scatter(go))
    dq, dk, dv = attn_bwd(qkv, lens, dmx, o, lse, trees)
    dx, st2, gq = qkv_bwd(x, ha, dq, dk, dv, dmid, mod, gain_a, wq)
    gq = finish(scatter(gq))
    dmod = jnp.concatenate([st2[:, 0], st2[:, 1], st[:, 0], st[:, 1], st[:, 2], st[:, 3]], axis=1)
    dmods = lax.all_gather(dmod, both, axis=0, tiled=True)
    conds = lax.all_gather(cond, both, axis=0, tiled=True)
    me = lax.axis_index("shard")
    mine = lambda v: lax.dynamic_slice_in_dim(v, me * (v.shape[-1] // shards), v.shape[-1] // shards, v.ndim - 1)
    dmine = mine(dmods)
    grad_w_mod = jnp.dot(conds.astype(F32).T, dmine, precision=HIGHEST)
    grad_b_mod = jnp.sum(dmine, axis=0)
    sums = lax.psum(jnp.concatenate([st2[:, 2].sum(0), st[:, 4].sum(0), gb[0], st[:, 5].sum(0)]), both)
    ga = mine(sums[:D])
    gm = mine(sums[D:2 * D])
    gbu = mine(sums[2 * D:2 * D + FF])
    gbd = mine(sums[2 * D + FF:])
    return (out.reshape(tokens.shape), dx.reshape(tokens.shape), ga, gq, go, gm, gu, gbu, gd, gbd, grad_w_mod, grad_b_mod)


def solution(mesh):
    rows = P(None, ("rep", "shard"), None, None)
    vec, mat, col = P("shard"), P("shard", None), P(None, "shard")
    in_specs = (rows, rows, P(None, ("rep", "shard")), P(None, ("rep", "shard"), None),
                vec, mat, mat, vec, mat, vec, mat, vec, col, vec)
    out_specs = (rows, rows, vec, mat, mat, vec, mat, vec, mat, vec, col, vec)
    return jax.shard_map(functools.partial(per_device, mesh.shape["shard"]), mesh=mesh,
                         in_specs=in_specs, out_specs=out_specs, check_vma=False)
```

time: 1600 us -> 694 us (0.43)
  matrix products: 484 us -> 2.96 us
  waiting for transfers between devices: 619 us -> 287 us
  Pallas kernels: 0 us -> 252 us
  other arithmetic: 203 us -> 7.96 us
  local copies, waits for them, and re-layouts: 115 us -> 13.7 us
  blocking collectives: 152 us -> 108 us
    dot_general x50 -> x2, matrix products: 484 us -> 2.96 us  [the longest x1 1.73 us: per_device(): jnp.dot(cond, mod_w, preferred_element_type=F32) + mod_b]
    reduce_scatter x8 -> x4, waiting for transfers between devices: 538 us -> 151 us  [per_device(): lax.psum_scatter(g, 'shard', scatter_dimension=0, tiled=True)]
    pallas_call x0 -> x7, Pallas kernels: none -> 252 us  [the longest x1 71.7 us: mlp_core(): pl.pallas_call(functools.partial(core_kernel, RB), grid=(FF // C,), in_sp...]
    while x4 -> x0, blocking collectives: 115 us -> none
    convert_element_type x35 -> x6, other arithmetic: 94.7 us -> 6.24 us  [the longest x4 6.1 us: per_device(): finish = lambda g: lax.psum(g, 'rep').astype(F32)]
    reduce_sum x20 -> x2, other arithmetic: 75.2 us -> 0.75 us  [the longest x1 0.72 us: per_device(): grad_b_mod = jnp.sum(dmine, axis=0)]
    all_gather x10 -> x6, waiting for transfers between devices: 22.6 us -> 90.7 us  [the longest x5 90.7 us: per_device(): gather = lambda w, axis=0: lax.all_gather(w, 'shard', axis=axis, tiled=True)]
    while x379 -> x0, local copies, waits for them, and re-layouts: 56.9 us -> none
  transfers between devices with their start and end apart: 21 -> 11, of which waited for: 11 -> 7; matrix products, arithmetic and copies ran while one was open for 23% -> 3% of each run, Pallas kernels for 0% -> 23%
where the time goes in v1:
time: 694 us; the launch traced here: 687 us
  waiting for transfers between devices  287 us (41%)
  Pallas kernels  252 us (36%)
  blocking collectives  108 us (16%)
  between operations  15.2 us (2%)
  local copies, waits for them, and re-layouts  13.7 us (2%)
  other arithmetic  7.96 us (1%)
    reduce_scatter x4, waiting for transfers between devices, per_device(): lax.psum_scatter(g, 'shard', scatter_dimension=0, tiled=True)  151 us
    all_gather x5, waiting for transfers between devices, per_device(): gather = lambda w, axis=0: lax.all_gather(w, 'shard', axis=axis, tiled=True)  90.7 us
    pallas_call x1, Pallas kernels, mlp_core(): pl.pallas_call(functools.partial(core_kernel, RB), grid=(FF // C,), in_sp...  71.7 us
    pallas_call x1, Pallas kernels, attn_bwd(): pl.pallas_call(functools.partial(bwd_kernel, mode), grid_spec=gs, out_sha...  62.3 us
    psum x1, waiting for transfers between devices, per_device(): finish = lambda g: lax.psum(g, 'rep').astype(F32)  39.9 us
    all_gather x1, blocking collectives, per_device(): conds = lax.all_gather(cond, both, axis=0, tiled=True)  39 us
    psum x1, blocking collectives, per_device(): lax.psum(jnp.concatenate([st2[:, 2].sum(0), st[:, 4].sum(0), gb[0], st[:,...  37.8 us
    pallas_call x1, Pallas kernels, attn_fwd(): pl.pallas_call(fwd_kernel, grid_spec=gs, out_shape=[jax.ShapeDtypeStruct(...  37 us
  transfers between devices with their start and end apart: 11, of which 7 were waited for; matrix products, arithmetic and copies ran while one was open for 3% of the time, Pallas kernels for 23%

profile of v1, /device:TPU:0, one launch (start us, length us, event | category | flops | bytes accessed | tf_op | source)
XLA Modules:
  0.0 686.8 jit_solution(4188985617501640986)
XLA Ops:
  7.2 0.7 all-gather.10.cloned.1.call-update
  8.0 0.7 all-gather.12.cloned.1.call-update
  8.7 0.7 all-gather.14.cloned.1.call-update
  10.6 1.2 dynamic-slice
  12.5 3.5 concatenate.13
  16.3 30.8 %all-reduce = bf16[9984]{0:T(1024)(128)(2,1)S(1)} all-reduce(bf16[9984]{0:T(1024)(128)(2,1)S(1)} %dynamic-update-slice), channel_id=2, replica_groups=mesh['rep'=4,'shard'=8] {'shard'}, use_global_device_ids=true, to_apply=%add | all-reduce | flops 9984 | bytes 39936
  50.9 1.7 convolution_add_fusion
  53.3 24.7 %all-gather.12.cloned.1.call-done.w_ref = bf16[768,2304]{1,0:T(8,128)(2,1)} async-done(((bf16[96,2304]{1,0:T(8,128)(2,1)}), bf16[768,2304]{1,0:T(8,128)(2,1)}) %all-gather.12.cloned.1.call-update) | async-done | bytes 3538960 | tf_op jit(solution)/shard_map/all_gather | solution.py:335
  78.0 13.6 %qkv_fwd.1 = (bf16[2048,768]{1,0:T(8,128)(2,1)}, bf16[2048,2304]{1,0:T(8,128)(2,1)}) custom-call(bf16[2048,768]{1,0:T(8,128)(2,1)} %bitcast.46, f32[2,6,768]{2,1,0:T(8,128)} %reshape.121.mod_ref, f32[1,768]{1,0:T(1,128)} %reshape.125.gain_ref, bf16[768,2304]{1,0:T(8,128)(2,1)} %all-gather.12.cloned.1.call-done.w_ref), custom_call_target="tpu_custom_call" | custom-call | tf_op jit(solution)/shard_map/qkv_fwd/pallas_call | solution.py:165
  91.6 37.0 %attn_fwd.1 = (bf16[2048,768]{1,0:T(8,128)(2,1)}, f32[2048,128]{1,0:T(8,128)}) custom-call(s32[2,12]{1,0:T(2,128)} %bitcast.56, bf16[2048,2304]{1,0:T(8,128)(2,1)} %get-tuple-element.35.q_ref.k_ref.v_ref, bf16[2048,2304]{1,0:T(8,128)(2,1)} %get-tuple-element.35.q_ref.k_ref.v_ref, bf16[2048,2304]{1,0:T(8,128)(2,1)} %get-tuple-element.35.q_ref.k_ref.v_ref), custom_call_target="tpu_custom_call" | custom-call | tf_op jit(solution)/shard_map/attn_fwd/pallas_call | solution.py:71
  128.6 10.7 %mlp_pre.1 = (f32[2048,768]{1,0:T(8,128)}, bf16[2048,768]{1,0:T(8,128)(2,1)}, bf16[2048,768]{1,0:T(8,128)(2,1)}) custom-call(bf16[2048,768]{1,0:T(8,128)(2,1)} %bitcast.47, bf16[2048,768]{1,0:T(8,128)(2,1)} %bitcast.50, bf16[2048,768]{1,0:T(8,128)(2,1)} %get-tuple-element.36.mx_ref.o_ref, f32[2,6,768]{2,1,0:T(8,128)} %reshape.121.mod_ref, ...), custom_call_target="tpu_custom_call" | custom-call | tf_op jit(solution)/shard_map/mlp_pre/pallas_call | solution.py:184
  139.3 14.4 %all-gather.16.cloned.1.call-done.wu_ref = bf16[768,3072]{1,0:T(8,128)(2,1)} async-done(((bf16[96,3072]{1,0:T(8,128)(2,1)}), bf16[768,3072]{1,0:T(8,128)(2,1)}) %all-gather.16.cloned.1.call-update) | async-done | bytes 4718608 | tf_op jit(solution)/shard_map/all_gather | solution.py:335
  153.7 51.5 %all-gather.18.cloned.1.call-done.wd_ref = bf16[3072,768]{1,0:T(8,128)(2,1)} async-done(((bf16[384,768]{1,0:T(8,128)(2,1)}), bf16[3072,768]{1,0:T(8,128)(2,1)}) %all-gather.18.cloned.1.call-update) | async-done | bytes 4718608 | tf_op jit(solution)/shard_map/all_gather | solution.py:335
  205.2 71.7 %mlp_core.1 = (f32[2048,768]{1,0:T(8,128)}, f32[2048,768]{1,0:T(8,128)}, bf16[768,3072]{1,0:T(8,128)(2,1)}, f32[1,3072]{1,0:T(1,128)}, bf16[3072,768]{1,0:T(8,128)(2,1)}) custom-call(bf16[2048,768]{1,0:T(8,128)(2,1)} %get-tuple-element.38.hm_ref, bf16[2048,768]{1,0:T(8,128)(2,1)} %get-tuple-element.39.dd_ref, ...), custom_call_target="tpu_custom_call" | custom-call | tf_op jit(solution)/shard_map/mlp_core/pallas_call | solution.py:221
  276.9 23.6 %mlp_post.1 = (bf16[2048,768]{1,0:T(8,128)(2,1)}, f32[2048,768]{1,0:T(8,128)}, bf16[2048,768]{1,0:T(8,128)(2,1)}, f32[2,8,768]{2,1,0:T(8,128)}, bf16[768,768]{1,0:T(8,128)(2,1)}) custom-call(bf16[2048,768]{1,0:T(8,128)(2,1)} %bitcast.48, bf16[2048,768]{1,0:T(8,128)(2,1)} %bitcast.51, bf16[2048,768]{1,0:T(8,128)(2,1)} %get-tuple-element.36.mx_ref.o_ref, ...), custom_call_target="tpu_custom_call" | custom-call | tf_op jit(solution)/shard_map/mlp_post/pallas_call | solution.py:270
  300.6 62.3 %attn_bwd.1 = (bf16[2048,768]{1,0:T(8,128)(2,1)}, bf16[2048,768]{1,0:T(8,128)(2,1)}, bf16[2048,768]{1,0:T(8,128)(2,1)}) custom-call(s32[2,12]{1,0:T(2,128)} %bitcast.57, bf16[2048,2304]{1,0:T(8,128)(2,1)} %get-tuple-element.35.q_ref.k_ref.v_ref, bf16[2048,2304]{1,0:T(8,128)(2,1)} %get-tuple-element.35.q_ref.k_ref.v_ref, ...), custom_call_target="tpu_custom_call" | custom-call | tf_op jit(solution)/shard_map/attn_bwd/pallas_call | solution.py:143
  362.9 33.3 %qkv_bwd.1 = (bf16[2048,768]{1,0:T(8,128)(2,1)}, f32[2,8,768]{2,1,0:T(8,128)}, bf16[768,2304]{1,0:T(8,128)(2,1)}) custom-call(bf16[2048,768]{1,0:T(8,128)(2,1)} %bitcast.49, bf16[2048,768]{1,0:T(8,128)(2,1)} %get-tuple-element.43.ha_ref, bf16[2048,768]{1,0:T(8,128)(2,1)} %get-tuple-element.46.dq_ref, bf16[2048,768]{1,0:T(8,128)(2,1)} %get-tuple-element.47.dk_ref, ...), custom_call_target="tpu_custom_call" | custom-call | tf_op jit(solution)/shard_map/qkv_bwd/pallas_call | solution.py:309
  396.3 0.7 reduce-scatter.11.cloned.1.call-update
  397.1 0.7 reduce-scatter.9.cloned.1.call-update
  399.0 39.9 %reduce-scatter.5.cloned.1.call-done = bf16[96,2304]{1,0:T(8,128)(2,1)} async-done(((bf16[768,2304]{1,0:T(8,128)(2,1)}), bf16[96,2304]{1,0:T(8,128)(2,1)}) %reduce-scatter.5.cloned.1.call-update) | async-done | bytes 442384 | tf_op jit(solution)/shard_map/reduce_scatter | solution.py:355
  438.9 55.7 %reduce-scatter.11.cloned.1.call-done = bf16[384,768]{1,0:T(8,128)(2,1)} async-done(((bf16[3072,768]{1,0:T(8,128)(2,1)}), bf16[384,768]{1,0:T(8,128)(2,1)}) %reduce-scatter.11.cloned.1.call-update) | async-done | bytes 589840 | tf_op jit(solution)/shard_map/reduce_scatter | solution.py:355
  494.6 55.7 %reduce-scatter.9.cloned.1.call-done = bf16[96,3072]{1,0:T(8,128)(2,1)} async-done(((bf16[768,3072]{1,0:T(8,128)(2,1)}), bf16[96,3072]{1,0:T(8,128)(2,1)}) %reduce-scatter.9.cloned.1.call-update) | async-done | bytes 589840 | tf_op jit(solution)/shard_map/reduce_scatter | solution.py:355
  550.4 39.0 %all-gather.1 = bf16[32,2,128]{2,1,0:T(2,128)(2,1)S(1)} all-gather(bf16[1,2,128]{2,1,0:T(2,128)(2,1)S(1)} %fusion.9), channel_id=1, replica_groups=mesh['rep'=4,'shard'=8] {'rep','shard'}, dimensions={0}, use_global_device_ids=true | all-gather | bytes 16896 | tf_op jit(solution)/shard_map/all_gather | solution.py:366
  589.5 37.8 %psum.35 = f32[5376]{0:T(1024)S(1)} all-reduce(f32[5376]{0:T(1024)S(1)} %pad_maximum_fusion), channel_id=1, replica_groups=mesh['rep'=4,'shard'=8] {'rep','shard'}, use_global_device_ids=true, to_apply=%region_3.4 | all-reduce | flops 5376 | bytes 43008 | tf_op jit(solution)/shard_map/psum | solution.py:372
  629.7 2.1 reshape.136
  631.8 0.7 dynamic-slice_reduce_fusion
  632.5 1.2 fusion
  633.8 39.9 %all-reduce.4.cloned.1.call-done = (bf16[96,2304]{1,0:T(8,128)(2,1)}, bf16[96,768]{1,0:T(8,128)(2,1)}, bf16[96,3072]{1,0:T(8,128)(2,1)}, bf16[384,768]{1,0:T(8,128)(2,1)}) async-done(((bf16[96,2304]{1,0:T(8,128)(2,1)}, bf16[96,768]{1,0:T(8,128)(2,1)}, bf16[96,3072]{1,0:T(8,128)(2,1)}, bf16[384,768]{1,0:T(8,128)(2,1)}), (bf16[96,2304]{1,0:T(8,128)(2,1)}, bf16[96,768]{1,0:T(8,128)(2,1)}, ...) | async-done | bytes 1769488 | tf_op jit(solution)/shard_map/psum | solution.py:356
  673.7 2.2 convert_element_type.65
  676.0 2.2 convert_element_type.66
  678.1 1.0 convert_element_type.63
  679.1 0.7 convert_element_type.64
  (66 shorter events, 9.9 us)
Async XLA Ops:
  7.2 43.7 %all-gather.10.cloned.1.call-start = ((), (), s32[]{:S(2)}) async-start(), calls=%async_computation.4 | async-start | bytes 1327104 | tf_op jit(solution)/shard_map/all_gather | solution.py:335
  7.9 70.1 %all-gather.12.cloned.1.call-start = ((), (), s32[]{:S(2)}) async-start(), calls=%async_computation.5 | async-start | bytes 3981312 | tf_op jit(solution)/shard_map/all_gather | solution.py:335
  8.7 119.9 %all-gather.14.cloned.1.call-start = ((), (), s32[]{:S(2)}) async-start(), calls=%async_computation.6 | async-start | bytes 1327104 | tf_op jit(solution)/shard_map/all_gather | solution.py:335
  9.4 144.3 %all-gather.16.cloned.1.call-start = ((), (), s32[]{:S(2)}) async-start(), calls=%async_computation.7 | async-start | bytes 5308416 | tf_op jit(solution)/shard_map/all_gather | solution.py:335
  10.0 195.2 %all-gather.18.cloned.1.call-start = ((), (), s32[]{:S(2)}) async-start(), calls=%async_computation.8 | async-start | bytes 5308416 | tf_op jit(solution)/shard_map/all_gather | solution.py:335
  10.6 388.4 %reduce-scatter.7.cloned.1.call-start = ((), (), s32[]{:S(2)}) async-start(), calls=%async_computation.10 | async-start | bytes 1327104 | tf_op jit(solution)/shard_map/reduce_scatter | solution.py:355
  300.5 138.3 %reduce-scatter.5.cloned.1.call-start = ((), (), s32[]{:S(2)}) async-start(), calls=%async_computation.9 | async-start | bytes 3981312 | tf_op jit(solution)/shard_map/reduce_scatter | solution.py:355
  396.2 98.4 %reduce-scatter.11.cloned.1.call-start = ((), (), s32[]{:S(2)}) async-start(), calls=%async_computation.12 | async-start | bytes 5308416 | tf_op jit(solution)/shard_map/reduce_scatter | solution.py:355
  397.0 1.1 copy-start.3
  397.0 1.1 copy-start.2
  397.0 153.3 %reduce-scatter.9.cloned.1.call-start = ((), (), s32[]{:S(2)}) async-start(), calls=%async_computation.11 | async-start | bytes 5308416 | tf_op jit(solution)/shard_map/reduce_scatter | solution.py:355
  397.1 192.4 %copy-start.5 = (f32[1,3072]{1,0:T(1,128)S(1)}, f32[1,3072]{1,0:T(1,128)}, u32[]{:S(2)}) copy-start(f32[1,3072]{1,0:T(1,128)} %get-tuple-element.53) | copy-start | bytes 36868
  397.7 232.0 %all-gather.20.cloned.1.call-start = ((), (), s32[]{:S(2)}) async-start(), calls=%async_computation.13 | async-start | bytes 1216512 | tf_op jit(solution)/shard_map/all_gather | solution.py:365
  398.2 0.6 copy-start.4
  398.9 274.8 %all-reduce.4.cloned.1.call-start = ((), (), s32[]{:S(2)}) async-start(), calls=%async_computation.14 | async-start | bytes 3538944 | tf_op jit(solution)/shard_map/psum | solution.py:356
  673.7 4.4 copy-start
  673.7 5.4 copy-start.1
Sparse Core Ops, SparseCore 0:
  9.6 25.6 all-gather.9
  37.0 40.9 all-gather.11
  79.7 21.6 all-gather.13
  102.8 50.8 all-gather.15
  155.2 49.9 all-gather.17
  300.6 31.7 reduce-scatter.6
  396.4 42.4 reduce-scatter.4
  441.2 53.3 reduce-scatter.10
  496.9 53.3 reduce-scatter.8
  553.8 52.5 all-gather.19
  609.8 63.9 all-reduce.3
